TPU v7x, 128 devices: a whole 4x4x4 slice. The times are simulated.
128 devices in a mesh: src: 4 (over z_hi, core), rcv: 32 (over y, z_lo, x).
Axes of the slice: x: 4, y: 4, z: 4 (z_hi: 2, z_lo: 2; z = z_hi * 2 + z_lo), core: 2. Of those that a mesh axis runs over, the one named last changes fastest.
Arguments:
- traces: bfloat16 [4096, 16, 2000], P('rcv', 'src')
- src_index: int32 [256], P('src'), may hold values from 0 to 4095, as said below
- quality: int32 [4096, 16], P('rcv'), may hold values 0 or 1
Outputs:
- xcorr: float32 [256, 201, 4096], P('src', None, 'rcv')
Inputs may be any that keep to these rules, and one draw needn't show every extreme that they name: `src_index`: the source numbered j within each group of 64 sources lies in receiver block j mod 32, among channels (j mod 32) * 128 up to that plus 128 - 1.
All inputs are finite; a program needn't handle non-finite values. No bound on the sum of `quality` on one device may be relied on, other than what follows from the above.
Results may differ from a plain program's by a relative error of at most 0.0067.
Values may be sent and summed in bfloat16 or wider, within the bound.
No kernel may reach another device: no remote copies, remote signals or barrier semaphores. Data moves between devices by JAX's collectives and lax.ppermute only.
A program may use at most 576 MiB of HBM per device.

v0:
```python
import math
import jax
import jax.numpy as jnp
from jax import lax
from jax.sharding import PartitionSpec as P

LAGH = 100


def make_tables(length):
    half = length // 2
    bins = jnp.arange(1, half + 1, dtype=jnp.int32)
    times = jnp.arange(length, dtype=jnp.int32)
    phase = (times[:, None] * bins[None, :] % length).astype(jnp.float32) * (2.0 * math.pi / length)
    forward = jnp.concatenate([jnp.cos(phase), -jnp.sin(phase)], axis=1).astype(jnp.bfloat16)
    lagvals = jnp.arange(-LAGH, LAGH + 1, dtype=jnp.int32)
    phase_lag = (bins[:, None] * lagvals[None, :] % length).astype(jnp.float32) * (
        2.0 * math.pi / length
    )
    weights = jnp.where(bins == half, 1.0, 2.0).astype(jnp.float32)[:, None] / jnp.sqrt(
        jnp.float32(half)
    )
    inverse = jnp.concatenate(
        [weights * jnp.cos(phase_lag), -weights * jnp.sin(phase_lag)], axis=0
    ).astype(jnp.bfloat16)
    return (forward, inverse)


def whiten(samples, forward):
    length = samples.shape[2]
    half = length // 2
    spec = jnp.dot(samples.reshape(-1, length), forward, preferred_element_type=jnp.float32)
    real_part = spec[:, :half]
    imag_part = spec[:, half:]
    power = real_part * real_part + imag_part * imag_part
    level = 0.5 * jnp.sqrt(jnp.mean(power, axis=1, keepdims=True) + 1e-06)
    denom = jnp.maximum(jnp.sqrt(power), level)
    white = jnp.concatenate([real_part / denom, imag_part / denom], axis=1).astype(jnp.bfloat16)
    return white.reshape(samples.shape[0], samples.shape[1], length)


def on_device(traces, src_index, quality):
    rows, seg_local, length = traces.shape
    half = length // 2
    nsrc = src_index.shape[0]
    seg_all = quality.shape[1]
    forward, inverse = make_tables(length)
    white_local = whiten(traces, forward)
    white_all = lax.all_gather(white_local, "src", axis=1, tiled=True)
    qual = quality.astype(jnp.bfloat16)
    first_channel = lax.axis_index("rcv") * rows
    onehot = (
        src_index[:, None] == first_channel + jnp.arange(rows, dtype=jnp.int32)[None, :]
    ).astype(jnp.bfloat16)
    found = jnp.dot(onehot, white_all.reshape(rows, -1), preferred_element_type=jnp.float32)
    flags = jnp.dot(onehot, qual, preferred_element_type=jnp.float32)
    found, flags = (
        lax.psum(found.astype(jnp.bfloat16), "rcv").astype(jnp.float32),
        lax.psum(flags.astype(jnp.bfloat16), "rcv").astype(jnp.float32),
    )
    srcw = found.reshape(nsrc, seg_all, length).astype(jnp.bfloat16)
    msrc = flags.astype(jnp.bfloat16)
    count = jnp.dot(msrc, qual.T, preferred_element_type=jnp.float32)
    recv = white_all * qual[:, :, None]
    recv_re = recv[:, :, :half]
    recv_im = recv[:, :, half:]
    left_all = srcw * msrc[:, :, None]
    group = 8
    left_blocks = left_all.reshape(nsrc // group, group, seg_all, length)

    def one_block(left):
        left_re = left[:, :, :half]
        left_im = left[:, :, half:]
        pre = jnp.einsum("isk,jsk->ijk", left_re, recv_re, preferred_element_type=jnp.float32)
        pre = pre + jnp.einsum("isk,jsk->ijk", left_im, recv_im, preferred_element_type=jnp.float32)
        pim = jnp.einsum("isk,jsk->ijk", left_im, recv_re, preferred_element_type=jnp.float32)
        pim = pim - jnp.einsum("isk,jsk->ijk", left_re, recv_im, preferred_element_type=jnp.float32)
        cross = jnp.concatenate([pre, pim], axis=2).astype(jnp.bfloat16)
        return jnp.einsum("ijk,kt->itj", cross, inverse, preferred_element_type=jnp.float32)

    lagged = lax.map(one_block, left_blocks)
    lagged = lagged.reshape(nsrc, 2 * LAGH + 1, rows)
    return lagged / jnp.maximum(count, 1.0)[:, None, :]


def solution(mesh):
    return jax.shard_map(
        on_device,
        mesh=mesh,
        in_specs=(P("rcv", "src", None), P("src"), P("rcv", None)),
        out_specs=P("src", None, "rcv"),
        check_vma=False,
    )
```

profile of v0, /device:TPU:1, one launch (start us, length us, event | category | flops | bytes accessed | tf_op | source)
XLA Modules:
  0.0 1214.9 jit_solution(14916867752042446205)
XLA Ops:
  6.5 35.3 %cosine_convert_fusion = (bf16[2000,1000]{1,0:T(8,128)(2,1)}, bf16[2000,1000]{1,0:T(8,128)(2,1)}) fusion(s32[1000]{0:T(1024)S(1)} %iota_add_fusion), kind=kLoop, calls=%fused_computation.36 | loop fusion | flops 24000000 | bytes 8004000 | tf_op jit(solution)/shard_map/convert.10
  41.9 3.4 copy.17
  47.6 10.1 fusion.37
  62.0 2.8 pad_maximum_fusion.1
  64.8 3.0 copy.20
  67.9 65.1 %all-gather.2.cloned.1.call-done = bf16[128,16,2000]{0,2,1:T(8,128)(2,1)} async-done(((bf16[128,4,2000]{0,2,1:T(8,128)(2,1)}), bf16[128,16,2000]{0,2,1:T(8,128)(2,1)}) %all-gather.2.cloned.1.call-update) | async-done | bytes 8192016 | tf_op jit(solution)/shard_map/all_gather | solution.py:49
  133.0 8.3 convolution_convert_fusion
  141.2 9.6 convert_element_type.35
  150.9 31.0 %copy.21 = bf16[8,8,16,2000]{2,1,3,0:T(8,128)(2,1)} copy(bf16[8,8,16,2000]{3,2,1,0:T(8,128)(2,1)} %convert_element_type.35) | data formatting | bytes 8192000 | tf_op jit(solution)/shard_map/convert_element_type | solution.py:61
  182.8 76.6 %psum.15 = bf16[64,16]{0,1:T(8,128)(2,1)S(1)} all-reduce(bf16[64,16]{0,1:T(8,128)(2,1)S(1)} %convolution_convert_fusion.1), channel_id=1, replica_groups=mesh['src'=4,'rcv'=32] {'rcv'}, use_global_device_ids=true, to_apply=%region_2.3 | all-reduce | flops 1024 | bytes 4096 | tf_op jit(solution)/shard_map/psum | solution.py:59
  260.3 3.7 multiply_convert_fusion.1
  265.2 7.3 broadcast_multiply_fusion.1
  272.5 3.8 fusion.54
  281.3 611.0 %all-reduce.2.cloned.1.call-done = bf16[8,8,16,2000]{2,1,3,0:T(8,128)(2,1)} async-done(((bf16[8,8,16,2000]{2,1,3,0:T(8,128)(2,1)}), bf16[8,8,16,2000]{2,1,3,0:T(8,128)(2,1)}) %all-reduce.2.cloned.1.call-update) | async-done | bytes 4096016 | tf_op jit(solution)/shard_map/psum | solution.py:58
  892.3 22.5 %broadcast_multiply_fusion = bf16[8,8,16,2000]{2,1,3,0:T(8,128)(2,1)} fusion(bf16[8,8,16,2000]{2,1,3,0:T(8,128)(2,1)} %all-reduce.2.cloned.1.call-done, bf16[8,8,16]{2,1,0:T(8,128)(2,1)S(1)} %bitcast.91), kind=kLoop, calls=%fused_computation.27 | loop fusion | flops 2048000 | bytes 8194048 | tf_op jit(solution)/shard_map/mul | solution.py:67
  914.8 285.8 %while.10 = (s32[]{:T(128)}, f32[8,8,201,128]{3,1,0,2:T(8,128)}, bf16[8,8,16,2000]{2,1,3,0:T(8,128)(2,1)}, bf16[128,16,1000]{0,1,2:T(8,128)(2,1)}, bf16[128,16,1...) while((s32[]{:T(128)}, f32[8,8,201,128]{3,1,0,2:T(8,128)}, ...), condition=%wide.region_4.5_spmd, body=%wide.region_3.4_spmd.sunk | while | flops 960512000 | bytes 119130632 | solution.py:81
  923.0 2.5 fusion.113
  934.2 14.2 %pad_maximum_fusion.4 = bf16[8,128,2000]{1,0,2:T(8,128)(2,1)S(1)} fusion(bf16[8,128,1000]{1,0,2:T(8,128)(2,1)S(1)} %copy-done, bf16[8,128,1000]{1,0,2:T(8,128)(2,1)S(1)} %fusion.117), kind=kLoop, calls=%fused_computation.clone.1 | loop fusion | flops 2048000 | bytes 8192000 | tf_op jit(solution)/shard_map/while/body/eval_jaxpr/concatenate | solution.py:78
  958.7 2.5 fusion.113
  969.9 14.2 %pad_maximum_fusion.4 = bf16[8,128,2000]{1,0,2:T(8,128)(2,1)S(1)} fusion(bf16[8,128,1000]{1,0,2:T(8,128)(2,1)S(1)} %copy-done, bf16[8,128,1000]{1,0,2:T(8,128)(2,1)S(1)} %fusion.117), kind=kLoop, calls=%fused_computation.clone.1 | loop fusion | flops 2048000 | bytes 8192000 | tf_op jit(solution)/shard_map/while/body/eval_jaxpr/concatenate | solution.py:78
  994.4 2.5 fusion.113
  1005.5 14.2 %pad_maximum_fusion.4 = bf16[8,128,2000]{1,0,2:T(8,128)(2,1)S(1)} fusion(bf16[8,128,1000]{1,0,2:T(8,128)(2,1)S(1)} %copy-done, bf16[8,128,1000]{1,0,2:T(8,128)(2,1)S(1)} %fusion.117), kind=kLoop, calls=%fused_computation.clone.1 | loop fusion | flops 2048000 | bytes 8192000 | tf_op jit(solution)/shard_map/while/body/eval_jaxpr/concatenate | solution.py:78
  1030.1 2.5 fusion.113
  1041.3 14.2 %pad_maximum_fusion.4 = bf16[8,128,2000]{1,0,2:T(8,128)(2,1)S(1)} fusion(bf16[8,128,1000]{1,0,2:T(8,128)(2,1)S(1)} %copy-done, bf16[8,128,1000]{1,0,2:T(8,128)(2,1)S(1)} %fusion.117), kind=kLoop, calls=%fused_computation.clone.1 | loop fusion | flops 2048000 | bytes 8192000 | tf_op jit(solution)/shard_map/while/body/eval_jaxpr/concatenate | solution.py:78
  1065.8 2.5 fusion.113
  1077.0 14.2 %pad_maximum_fusion.4 = bf16[8,128,2000]{1,0,2:T(8,128)(2,1)S(1)} fusion(bf16[8,128,1000]{1,0,2:T(8,128)(2,1)S(1)} %copy-done, bf16[8,128,1000]{1,0,2:T(8,128)(2,1)S(1)} %fusion.117), kind=kLoop, calls=%fused_computation.clone.1 | loop fusion | flops 2048000 | bytes 8192000 | tf_op jit(solution)/shard_map/while/body/eval_jaxpr/concatenate | solution.py:78
  1101.5 2.5 fusion.113
  1112.7 14.2 %pad_maximum_fusion.4 = bf16[8,128,2000]{1,0,2:T(8,128)(2,1)S(1)} fusion(bf16[8,128,1000]{1,0,2:T(8,128)(2,1)S(1)} %copy-done, bf16[8,128,1000]{1,0,2:T(8,128)(2,1)S(1)} %fusion.117), kind=kLoop, calls=%fused_computation.clone.1 | loop fusion | flops 2048000 | bytes 8192000 | tf_op jit(solution)/shard_map/while/body/eval_jaxpr/concatenate | solution.py:78
  1148.4 14.2 %pad_maximum_fusion.4 = bf16[8,128,2000]{1,0,2:T(8,128)(2,1)S(1)} fusion(bf16[8,128,1000]{1,0,2:T(8,128)(2,1)S(1)} %copy-done, bf16[8,128,1000]{1,0,2:T(8,128)(2,1)S(1)} %fusion.117), kind=kLoop, calls=%fused_computation.clone.1 | loop fusion | flops 2048000 | bytes 8192000 | tf_op jit(solution)/shard_map/while/body/eval_jaxpr/concatenate | solution.py:78
  1172.9 2.5 fusion.113
  1184.0 14.2 %pad_maximum_fusion.4 = bf16[8,128,2000]{1,0,2:T(8,128)(2,1)S(1)} fusion(bf16[8,128,1000]{1,0,2:T(8,128)(2,1)S(1)} %copy-done, bf16[8,128,1000]{1,0,2:T(8,128)(2,1)S(1)} %fusion.117), kind=kLoop, calls=%fused_computation.clone.1 | loop fusion | flops 2048000 | bytes 8192000 | tf_op jit(solution)/shard_map/while/body/eval_jaxpr/concatenate | solution.py:78
  1200.6 7.2 bitcast_divide_fusion
  (183 shorter events, 167.5 us)
Async XLA Ops:
  6.5 126.4 %all-gather.2.cloned.1.call-start = ((), (), s32[]{:S(2)}) async-start(), calls=%async_computation | async-start | bytes 10240000 | tf_op jit(solution)/shard_map/all_gather | solution.py:49
  64.8 68.2 %copy-start.7 = (s32[64]{0:T(128)S(1)}, s32[64]{0:T(128)}, u32[]{:S(2)}) copy-start(s32[64]{0:T(128)} %param.6) | copy-start | bytes 772
  67.8 824.5 %all-reduce.2.cloned.1.call-start = ((), (), s32[]{:S(2)}) async-start(), calls=%async_computation.1 | async-start | bytes 65536000 | tf_op jit(solution)/shard_map/psum | solution.py:58
  914.8 285.8 %copy-start.5 = (f32[64,128]{1,0:T(8,128)S(1)}, f32[64,128]{1,0:T(8,128)}, u32[]{:S(2)}) copy-start(f32[64,128]{1,0:T(8,128)} %convolution_maximum_fusion) | copy-start | bytes 98308
  915.0 3.4 copy-start.1
  919.6 3.4 copy-start.3
  929.2 3.4 copy-start.2
  934.2 14.3 %copy-start.4 = (bf16[2000,201]{0,1:T(8,128)(2,1)S(1)}, bf16[2000,201]{0,1:T(8,128)(2,1)}, u32[]{:S(2)}) copy-start(bf16[2000,201]{0,1:T(8,128)(2,1)} %get-tuple-element.122) | copy-start | bytes 2412004 | tf_op jit(solution)/shard_map/while
  950.7 3.4 copy-start.1
  955.3 3.4 copy-start.3
  964.9 3.4 copy-start.2
  969.9 14.3 %copy-start.4 = (bf16[2000,201]{0,1:T(8,128)(2,1)S(1)}, bf16[2000,201]{0,1:T(8,128)(2,1)}, u32[]{:S(2)}) copy-start(bf16[2000,201]{0,1:T(8,128)(2,1)} %get-tuple-element.122) | copy-start | bytes 2412004 | tf_op jit(solution)/shard_map/while
  986.4 3.4 copy-start.1
  991.0 3.4 copy-start.3
  1000.6 3.4 copy-start.2
  1005.5 14.3 %copy-start.4 = (bf16[2000,201]{0,1:T(8,128)(2,1)S(1)}, bf16[2000,201]{0,1:T(8,128)(2,1)}, u32[]{:S(2)}) copy-start(bf16[2000,201]{0,1:T(8,128)(2,1)} %get-tuple-element.122) | copy-start | bytes 2412004 | tf_op jit(solution)/shard_map/while
  1022.1 3.4 copy-start.1
  1026.7 3.4 copy-start.3
  1036.3 3.4 copy-start.2
  1041.3 14.3 %copy-start.4 = (bf16[2000,201]{0,1:T(8,128)(2,1)S(1)}, bf16[2000,201]{0,1:T(8,128)(2,1)}, u32[]{:S(2)}) copy-start(bf16[2000,201]{0,1:T(8,128)(2,1)} %get-tuple-element.122) | copy-start | bytes 2412004 | tf_op jit(solution)/shard_map/while
  1062.4 3.4 copy-start.3
  1072.0 3.4 copy-start.2
  1077.0 14.3 %copy-start.4 = (bf16[2000,201]{0,1:T(8,128)(2,1)S(1)}, bf16[2000,201]{0,1:T(8,128)(2,1)}, u32[]{:S(2)}) copy-start(bf16[2000,201]{0,1:T(8,128)(2,1)} %get-tuple-element.122) | copy-start | bytes 2412004 | tf_op jit(solution)/shard_map/while
  1098.1 3.4 copy-start.3
  1107.7 3.4 copy-start.2
  1112.7 14.3 %copy-start.4 = (bf16[2000,201]{0,1:T(8,128)(2,1)S(1)}, bf16[2000,201]{0,1:T(8,128)(2,1)}, u32[]{:S(2)}) copy-start(bf16[2000,201]{0,1:T(8,128)(2,1)} %get-tuple-element.122) | copy-start | bytes 2412004 | tf_op jit(solution)/shard_map/while
  1133.8 3.4 copy-start.3
  1143.4 3.4 copy-start.2
  1148.4 14.3 %copy-start.4 = (bf16[2000,201]{0,1:T(8,128)(2,1)S(1)}, bf16[2000,201]{0,1:T(8,128)(2,1)}, u32[]{:S(2)}) copy-start(bf16[2000,201]{0,1:T(8,128)(2,1)} %get-tuple-element.122) | copy-start | bytes 2412004 | tf_op jit(solution)/shard_map/while
  1169.5 3.4 copy-start.3
  1179.1 3.4 copy-start.2
  1184.0 14.3 %copy-start.4 = (bf16[2000,201]{0,1:T(8,128)(2,1)S(1)}, bf16[2000,201]{0,1:T(8,128)(2,1)}, u32[]{:S(2)}) copy-start(bf16[2000,201]{0,1:T(8,128)(2,1)} %get-tuple-element.122) | copy-start | bytes 2412004 | tf_op jit(solution)/shard_map/while
  (13 other events, 26.9 us)
Sparse Core Ops, SparseCore 0:
  67.9 64.9 all-gather.1
  182.0 710.2 all-reduce.1
where the time goes:
time: 1220 us; the launch traced here: 1210 us
  waiting for transfers between devices  676 us (55%)
  other arithmetic  195 us (16%)
  local copies, waits for them, and re-layouts  174 us (14%)
  matrix products  77.6 us (6%)
  blocking collectives  76.6 us (6%)
  between operations  13.9 us (1%)
    psum x1, waiting for transfers between devices, on_device(): lax.psum(found.astype(jnp.bfloat16), 'rcv').astype(jnp.float32)  611 us
    concatenate x8, other arithmetic, one_block(): cross = jnp.concatenate([pre, pim], axis=2).astype(jnp.bfloat16)  114 us
    psum x1, blocking collectives, on_device(): lax.psum(flags.astype(jnp.bfloat16), 'rcv').astype(jnp.float32)  76.6 us
    all_gather x1, waiting for transfers between devices, on_device(): white_all = lax.all_gather(white_local, 'src', axis=1, tiled=True)  65.1 us
    convert_element_type x2, local copies, waits for them, and re-layouts, on_device(): srcw = found.reshape(nsrc, seg_all, length).astype(jnp.bfloat16)  40.6 us
    another operation x3, other arithmetic  40 us
  transfers between devices with their start and end apart: 2, of which 2 were waited for; matrix products, arithmetic and copies ran while one was open for 2% of the time, Pallas kernels for 0%

commit v1 on v0

--- a/solution.py
+++ b/solution.py
@@ -46,7 +46,9 @@
     seg_all = quality.shape[1]
     forward, inverse = make_tables(length)
     white_local = whiten(traces, forward)
-    white_all = lax.all_gather(white_local, "src", axis=1, tiled=True)
+    white_all = jnp.concatenate(
+        lax.all_to_all(jnp.stack([white_local] * lax.axis_size("src")), "src", 0, 0), axis=1
+    )
     qual = quality.astype(jnp.bfloat16)
     first_channel = lax.axis_index("rcv") * rows
     onehot = (

time: 1220 us -> 876 us (0.72)
  the two profiles are of different devices: /device:TPU:1 before, /device:TPU:0 now
where the time goes in v1:
time: 876 us; the launch traced here: 873 us
  waiting for transfers between devices  298 us (34%)
  local copies, waits for them, and re-layouts  224 us (26%)
  matrix products  129 us (15%)
  other arithmetic  119 us (14%)
  blocking collectives  83.5 us (10%)
  between operations  13.5 us (2%)
    psum x1, waiting for transfers between devices, on_device(): lax.psum(found.astype(jnp.bfloat16), 'rcv').astype(jnp.float32)  206 us
    another operation x18, local copies, waits for them, and re-layouts  118 us
    all_to_all x1, waiting for transfers between devices, on_device(): lax.all_to_all(jnp.stack([white_local] * lax.axis_size('src')), 'src', 0, 0)  92.6 us
    psum x1, blocking collectives, on_device(): lax.psum(flags.astype(jnp.bfloat16), 'rcv').astype(jnp.float32)  83.5 us
    add x8, other arithmetic, one_block(): pre + jnp.einsum('isk,jsk->ijk', left_im, recv_im, preferred_element_type...  57.7 us
    another operation x3, other arithmetic  39 us
    dot_general x8, matrix products, one_block(): jnp.einsum('isk,jsk->ijk', left_im, recv_re, preferred_element_type=jnp.f...  28 us
    dot_general x8, matrix products, one_block(): jnp.einsum('isk,jsk->ijk', left_re, recv_re, preferred_element_type=jnp.f...  25.9 us
  transfers between devices with their start and end apart: 2, of which 2 were waited for; matrix products, arithmetic and copies ran while one was open for 4% of the time, Pallas kernels for 0%

profile of v1, /device:TPU:0, one launch (start us, length us, event | category | flops | bytes accessed | tf_op | source)
XLA Modules:
  0.0 872.8 jit_solution(7205208822910881751)
XLA Ops:
  12.3 34.3 %cosine_convert_fusion = (bf16[2000,1000]{1,0:T(8,128)(2,1)S(1)}, bf16[2000,1000]{1,0:T(8,128)(2,1)S(1)}) fusion(s32[1000]{0:T(1024)S(1)} %iota_add_fusion), kind=kLoop, calls=%fused_computation.25 | loop fusion | flops 24000000 | bytes 8004000 | tf_op jit(solution)/shard_map/convert.10
  74.3 92.6 %all-to-all-done = bf16[4,128,4,2000]{1,3,2,0:T(8,128)(2,1)} async-done(((bf16[4,128,4,2000]{1,3,2,0:T(8,128)(2,1)}), bf16[4,128,4,2000]{1,3,2,0:T(8,128)(2,1)}, u32[]{:S(2)}, u32[]{:S(2)}) %all-to-all-start) | async-done | bytes 8192032 | tf_op jit(solution)/shard_map/all_to_all | solution.py:50
  166.9 8.3 convolution_convert_fusion
  175.2 9.6 %convert_element_type.36 = bf16[8,8,16,2000]{3,2,1,0:T(8,128)(2,1)} reshape(bf16[64,32000]{1,0:T(8,128)(2,1)} %convolution_convert_fusion) | data formatting | bytes 8192000 | tf_op jit(solution)/shard_map/convert_element_type | solution.py:63
  185.7 83.5 %psum.15 = bf16[64,16]{0,1:T(8,128)(2,1)S(1)} all-reduce(bf16[64,16]{0,1:T(8,128)(2,1)S(1)} %convolution_convert_fusion.1), channel_id=1, replica_groups=mesh['src'=4,'rcv'=32] {'rcv'}, use_global_device_ids=true, to_apply=%region_2.3 | all-reduce | flops 1024 | bytes 4096 | tf_op jit(solution)/shard_map/psum | solution.py:61
  274.1 7.2 bitcast_multiply_fusion
  300.6 205.9 %all-reduce.2.cloned.1.call-done = bf16[8,8,16,2000]{3,2,1,0:T(8,128)(2,1)} async-done(((bf16[8,8,16,2000]{3,2,1,0:T(8,128)(2,1)}), bf16[8,8,16,2000]{3,2,1,0:T(8,128)(2,1)}) %all-reduce.2.cloned.1.call-update) | async-done | bytes 4096016 | tf_op jit(solution)/shard_map/psum | solution.py:60
  511.1 347.8 %while.10 = (s32[]{:T(128)}, f32[8,8,201,128]{3,1,0,2:T(8,128)}, bf16[8,8,16,2000]{3,2,1,0:T(8,128)(2,1)}, bf16[128,16,1000]{2,1,0:T(8,128)(2,1)}, bf16[128,16,1...) while((s32[]{:T(128)}, f32[8,8,201,128]{3,1,0,2:T(8,128)}, ...), condition=%wide.region_4.5_spmd, body=%wide.region_3.4_spmd.sunk | while | flops 966656000 | bytes 114890064 | solution.py:83
  516.8 7.3 copy.55
  524.1 7.3 copy.57
  545.0 7.2 fusion.90
  560.3 7.3 copy.55
  567.6 7.3 copy.57
  588.5 7.2 fusion.90
  603.8 7.3 copy.55
  611.0 7.3 copy.57
  632.0 7.2 fusion.90
  647.2 7.3 copy.55
  654.5 7.3 copy.57
  675.4 7.2 fusion.90
  690.7 7.3 copy.55
  698.0 7.3 copy.57
  718.9 7.2 fusion.90
  734.2 7.3 copy.55
  741.5 7.3 copy.57
  762.4 7.2 fusion.90
  777.6 7.3 copy.55
  784.9 7.3 copy.57
  805.9 7.2 fusion.90
  821.1 7.3 copy.55
  828.4 7.3 copy.57
  849.4 7.2 fusion.90
  (168 shorter events, 243.4 us)
Async XLA Ops:
  12.3 34.3 %copy-start.3 = (bf16[512,2000]{1,0:T(8,128)(2,1)S(1)}, bf16[512,2000]{1,0:T(8,128)(2,1)}, u32[]{:S(2)}) copy-start(bf16[512,2000]{1,0:T(8,128)(2,1)} %reshape.68) | copy-start | bytes 6144004
  68.4 98.4 %copy-start.6 = (s32[64]{0:T(128)S(1)}, s32[64]{0:T(128)}, u32[]{:S(2)}) copy-start(s32[64]{0:T(128)} %param.6) | copy-start | bytes 772
  68.4 98.4 %all-to-all-start = ((bf16[4,128,4,2000]{1,3,2,0:T(8,128)(2,1)}), bf16[4,128,4,2000]{1,3,2,0:T(8,128)(2,1)}, u32[]{:S(2)}, u32[]{:S(2)}) async-start(bf16[4,128,4,2000]{1,3,2,0:T(8,128)(2,1)} %stack.3), calls=%async_computation | async-start | bytes 16384000 | tf_op jit(solution)/shard_map/all_to_all | solution.py:50
  74.2 432.3 %all-reduce.2.cloned.1.call-start = ((), (), s32[]{:S(2)}) async-start(), calls=%async_computation.1 | async-start | bytes 8388608 | tf_op jit(solution)/shard_map/psum | solution.py:60
  184.8 0.7 copy-start.5
  511.1 347.8 %copy-start.4 = (f32[64,128]{1,0:T(8,128)S(1)}, f32[64,128]{1,0:T(8,128)}, u32[]{:S(2)}) copy-start(f32[64,128]{1,0:T(8,128)} %convolution_maximum_fusion) | copy-start | bytes 98308
  531.4 3.5 copy-start.1
  531.4 4.0 copy-start.2
  535.4 3.2 copy-start
  574.9 3.5 copy-start.1
  574.9 4.0 copy-start.2
  578.9 3.2 copy-start
  618.3 3.5 copy-start.1
  618.3 4.0 copy-start.2
  622.4 3.2 copy-start
  661.8 3.5 copy-start.1
  661.8 4.0 copy-start.2
  665.8 3.2 copy-start
  705.3 3.5 copy-start.1
  705.3 4.0 copy-start.2
  709.3 3.2 copy-start
  748.8 3.5 copy-start.1
  748.8 4.0 copy-start.2
  752.8 3.2 copy-start
  792.2 3.5 copy-start.1
  792.2 4.0 copy-start.2
  796.3 3.2 copy-start
  835.7 3.5 copy-start.1
  835.7 4.0 copy-start.2
  839.8 3.2 copy-start
Sparse Core Ops, SparseCore 0:
  184.9 321.5 all-reduce.1
